TPU v7x, 32 devices: a whole 2x2x4 slice. The times are simulated.
32 devices in a mesh: tiles: 2 (over x), space: 8 (over z, y), chan: 2 (over core).
Axes of the slice: x: 2, y: 2, z: 4, core: 2. Of those that a mesh axis runs over, the one named last changes fastest.
Arguments:
- volume: bfloat16 [32, 64, 32, 256], P(None, 'space', 'tiles', 'chan'), parts along dimension 2, may hold values from -6 to 6
- weight_one: bfloat16 [3, 3, 3, 256, 256], replicated, may hold values from -0.078125 to 0.078125
- bias_one: float32 [256], replicated, may hold values from -3 to 3
- weight_two: bfloat16 [3, 3, 3, 256, 256], replicated, may hold values from -0.078125 to 0.078125
- bias_two: float32 [256], replicated, may hold values from -3 to 3
Outputs:
- features: bfloat16 [32, 64, 32, 256], P('space', None, 'tiles', 'chan'), parts along dimension 2
There are 2 independent parts, one for each index of `tiles`. A program takes and returns all parts, laid end to end along the dimension named above; an argument that names none is the same for every part. Nothing has to cross between parts.
All inputs are finite; a program needn't handle non-finite values.
Results may differ from a plain program's by a relative error of at most 0.0044.
Values may be sent and summed in bfloat16 or wider, within the bound.
A program may use at most 128 MiB of HBM per device.

v0:
```python
import jax
import jax.numpy as jnp
from jax import lax
from jax.sharding import PartitionSpec as P


def padded(x, sides, width):
    for axis, dim in sides:
        devices, length = (lax.axis_size(axis), x.shape[dim])
        up = [(i, (i + 1) % devices) for i in range(devices - 1)]
        down = [(j, i) for i, j in up]
        last = lax.slice_in_dim(x, length - width, length, axis=dim)
        first = lax.slice_in_dim(x, 0, width, axis=dim)
        before = lax.ppermute(last, axis, up)
        after = lax.ppermute(first, axis, down)
        x = jnp.concatenate([before, x, after], axis=dim)
    return x


def convolve(field, kernel):
    return lax.conv_general_dilated(
        field[None],
        kernel,
        (1, 1, 1),
        ((0, 0), (1, 1), (1, 1)),
        dimension_numbers=("NDHWC", "DHWIO", "NDHWC"),
        preferred_element_type=jnp.float32,
    )[0]


def pad_layer(field):
    return padded(field, (("space", 0),), 1)


def body(volume, weight_one, bias_one, weight_two, bias_two):
    slab_data = lax.all_to_all(volume, "space", split_axis=0, concat_axis=1, tiled=True)
    share = slab_data.shape[3]
    offset = lax.axis_index("chan") * share

    def layer(field, kernel, bias):
        part_kernel = lax.dynamic_slice_in_dim(kernel, offset, share, 3)
        summed = lax.psum_scatter(
            convolve(field, part_kernel), "chan", scatter_dimension=3, tiled=True
        )
        return summed + lax.dynamic_slice_in_dim(bias, offset, share, 0)

    hidden = jnp.maximum(layer(pad_layer(slab_data), weight_one, bias_one), 0.0).astype(
        jnp.bfloat16
    )
    result = layer(pad_layer(hidden), weight_two, bias_two)
    return jnp.maximum(result, 0.0).astype(jnp.bfloat16)


def solution(mesh):
    return jax.shard_map(
        body,
        mesh=mesh,
        in_specs=(P(None, "space", "tiles", "chan"), P(), P(), P(), P()),
        out_specs=P("space", None, "tiles", "chan"),
        check_vma=False,
    )
```

profile of v0, /device:TPU:0, one launch (start us, length us, event | category | flops | bytes accessed | tf_op | source)
XLA Modules:
  0.0 152.2 jit_solution(18392344283605213715)
XLA Ops:
  6.5 33.3 %all_to_all.18 = bf16[32,8,16,128]{3,2,1,0:T(8,128)(2,1)S(1)} all-to-all(bf16[32,8,16,128]{3,2,1,0:T(8,128)(2,1)} %param.5), channel_id=1, replica_groups=mesh['tiles'=2,'space'=8,'chan'=2] {'space'}, dimensions={0} | all-to-all | bytes 2097152 | tf_op jit(solution)/shard_map/all_to_all | solution.py:36
  39.9 1.0 copy-done.2
  40.8 0.8 fusion.33
  41.7 4.1 %collective-permute-start = (bf16[1,64,16,128]{3,2,1,0:T(8,128)(2,1)}, bf16[1,64,16,128]{3,2,1,0:T(8,128)(2,1)}, u32[]{:S(2)}, u32[]{:S(2)}) collective-permute-start(bf16[1,64,16,128]{3,2,1,0:T(8,128)(2,1)} %bitcast.2), channel_id=1, source_target_pairs={{0,2},{2,4},{4,6},{6,8},{8,10},{10,12},{12,14},{1,3},{3,5},{5,7},{... | collective-permute-start | bytes 786440 | tf_op jit(solution)/shard_map/ppermute | solution.py:14
  45.7 1.3 collective-permute-start.1
  47.0 1.4 copy.14
  48.4 6.9 %collective-permute-done = bf16[1,64,16,128]{3,2,1,0:T(8,128)(2,1)} collective-permute-done((bf16[1,64,16,128]{3,2,1,0:T(8,128)(2,1)}, bf16[1,64,16,128]{3,2,1,0:T(8,128)(2,1)}, u32[]{:S(2)}, u32[]{:S(2)}) %collective-permute-start) | collective-permute-done | bytes 262176 | tf_op jit(solution)/shard_map/ppermute | solution.py:14
  55.4 1.2 maximum_bitcast_fusion
  57.4 1.5 %copy.17 = bf16[6,64,1,8,3,128]{5,3,4,1,0,2:T(8,128)(2,1)S(1)} copy(bf16[6,64,1,8,3,128]{5,1,4,3,0,2:T(8,128)(2,1)S(1)} %bitcast.31) | data formatting | bytes 4718592 | tf_op jit(solution)/shard_map/conv_general_dilated | solution.py:21
  59.6 13.5 %broadcast_select_fusion.1 = f32[4,64,8,3,256]{4,2,3,1,0:T(8,128)S(1)} fusion(pred[8,3]{0,1:T(4,128)(4,1)S(1)} %copy-done.6, bf16[6,64,1,7,2,128]{5,3,4,1,0,2:T(8,128)(2,1)S(1)} %slice.30, bf16[6,64,1,8,3,128]{5,3,4,1,0,2:T(8,128)(2,1)S(1)} %copy.17, bf16[3,3,3,256,256]{4,3,2,1,0:T(8,128)(2,1)S(1)} %copy-done, s32[]{:T(128)S(6)} %select_n.2), kind=kOutput, calls=%fused_computation.18 | convolution fusion | flops 10771759104 | bytes 11993604 | tf_op jit(solution)/shard_map/conv_general_dilated | solution.py:21
  73.0 1.9 %copy.18 = f32[4,64,8,3,256]{4,1,3,2,0:T(8,128)S(1)} copy(f32[4,64,8,3,256]{4,2,3,1,0:T(8,128)S(1)} %broadcast_select_fusion.1) | data formatting | bytes 12582912 | tf_op jit(solution)/shard_map/conv_general_dilated | solution.py:21
  75.0 2.4 %slice_bitcast_fusion.1 = f32[4,64,16,256]{3,1,2,0:T(8,128)} fusion(f32[4,64,1,24,256]{4,1,3,0,2:T(8,128)S(1)} %bitcast.28), kind=kLoop, calls=%fused_computation.4 | loop fusion | bytes 8388608 | tf_op jit(solution)/shard_map/squeeze | solution.py:21
  78.2 11.9 %reduce-scatter.3.cloned.1.call-done = f32[4,64,16,128]{3,1,2,0:T(8,128)} async-done(((f32[4,64,16,256]{3,1,2,0:T(8,128)}), f32[4,64,16,128]{3,1,2,0:T(8,128)}) %reduce-scatter.3.cloned.1.call-update) | async-done | bytes 2097168 | tf_op jit(solution)/shard_map/reduce_scatter | solution.py:42
  90.1 1.9 %maximum_convert_fusion.1 = bf16[4,64,16,128]{3,1,2,0:T(8,128)(2,1)S(1)} fusion(f32[4,64,16,128]{3,1,2,0:T(8,128)} %reduce-scatter.3.cloned.1.call-done, f32[128]{0:T(128)S(1)} %dynamic_slice.13), kind=kLoop, calls=%fused_computation.20 | loop fusion | flops 1572864 | bytes 3146240 | tf_op jit(solution)/shard_map/convert_element_type | solution.py:47
  92.0 3.8 %collective-permute-start.2 = (bf16[1,64,16,128]{3,1,2,0:T(8,128)(2,1)S(1)}, bf16[1,64,16,128]{3,1,2,0:T(8,128)(2,1)S(1)}, u32[]{:S(2)}, u32[]{:S(2)}) collective-permute-start(bf16[1,64,16,128]{3,1,2,0:T(8,128)(2,1)S(1)} %get-tuple-element.5), channel_id=1, source_target_pairs={{0,2},{2,4},{4,6},{6,8},{8,10},{10,12},{12,14},{1,3},{3,5},{5,7},{... | collective-permute-start | bytes 786440 | tf_op jit(solution)/shard_map/ppermute | solution.py:14
  95.8 1.5 collective-permute-start.3
  97.2 10.0 %collective-permute-done.2 = bf16[1,64,16,128]{3,1,2,0:T(8,128)(2,1)S(1)} collective-permute-done((bf16[1,64,16,128]{3,1,2,0:T(8,128)(2,1)S(1)}, bf16[1,64,16,128]{3,1,2,0:T(8,128)(2,1)S(1)}, u32[]{:S(2)}, u32[]{:S(2)}) %collective-permute-start.2) | collective-permute-done | bytes 262176 | tf_op jit(solution)/shard_map/ppermute | solution.py:14
  107.9 1.5 %copy.20 = bf16[6,64,1,8,3,128]{5,3,4,1,0,2:T(8,128)(2,1)S(1)} copy(bf16[6,64,1,8,3,128]{5,1,4,3,0,2:T(8,128)(2,1)S(1)} %bitcast.30) | data formatting | bytes 4718592 | tf_op jit(solution)/shard_map/conv_general_dilated | solution.py:21
  109.9 13.5 %broadcast_select_fusion = f32[4,64,8,3,256]{4,2,3,1,0:T(8,128)S(1)} fusion(pred[8,3]{0,1:T(4,128)(4,1)S(1)} %copy-done.6, bf16[6,64,1,7,2,128]{5,3,4,1,0,2:T(8,128)(2,1)S(1)} %slice.34, bf16[6,64,1,8,3,128]{5,3,4,1,0,2:T(8,128)(2,1)S(1)} %copy.20, bf16[3,3,3,256,256]{4,3,2,1,0:T(8,128)(2,1)S(1)} %copy-done.3, s32[]{:T(128)S(6)} %select_n.2), kind=kOutput, calls=%fused_computation.17 | convolution fusion | flops 10771759104 | bytes 11993604 | tf_op jit(solution)/shard_map/conv_general_dilated | solution.py:21
  123.3 1.9 %copy.21 = f32[4,64,8,3,256]{4,1,3,2,0:T(8,128)S(1)} copy(f32[4,64,8,3,256]{4,2,3,1,0:T(8,128)S(1)} %broadcast_select_fusion) | data formatting | bytes 12582912 | tf_op jit(solution)/shard_map/conv_general_dilated | solution.py:21
  125.3 2.4 %slice_bitcast_fusion = f32[4,64,16,256]{3,1,2,0:T(8,128)} fusion(f32[4,64,1,24,256]{4,1,3,0,2:T(8,128)S(1)} %bitcast.29), kind=kLoop, calls=%fused_computation.3 | loop fusion | bytes 8388608 | tf_op jit(solution)/shard_map/squeeze | solution.py:21
  128.5 13.4 %reduce-scatter.5.cloned.1.call-done = f32[4,64,16,128]{3,1,2,0:T(8,128)} async-done(((f32[4,64,16,256]{3,1,2,0:T(8,128)}), f32[4,64,16,128]{3,1,2,0:T(8,128)}) %reduce-scatter.5.cloned.1.call-update) | async-done | bytes 2097168 | tf_op jit(solution)/shard_map/reduce_scatter | solution.py:42
  141.8 1.9 %maximum_convert_fusion = bf16[4,64,16,128]{3,1,2,0:T(8,128)(2,1)S(1)} fusion(f32[4,64,16,128]{3,1,2,0:T(8,128)} %reduce-scatter.5.cloned.1.call-done, f32[128]{0:T(128)S(1)} %dynamic_slice.15), kind=kLoop, calls=%fused_computation.19 | loop fusion | flops 1572864 | bytes 3146240 | tf_op jit(solution)/shard_map/convert_element_type | solution.py:51
  143.7 1.7 %copy.22 = bf16[4,64,16,128]{3,2,1,0:T(8,128)(2,1)} copy(bf16[4,64,16,128]{3,1,2,0:T(8,128)(2,1)S(1)} %maximum_convert_fusion) | data formatting | bytes 2097152 | tf_op jit(solution)/shard_map/convert_element_type | solution.py:51
  (28 shorter events, 4.0 us)
Async XLA Ops:
  6.5 52.8 %copy-start = (bf16[3,3,3,256,256]{4,3,2,1,0:T(8,128)(2,1)S(1)}, bf16[3,3,3,256,256]{4,3,2,1,0:T(8,128)(2,1)}, u32[]{:S(2)}) copy-start(bf16[3,3,3,256,256]{4,3,2,1,0:T(8,128)(2,1)} %param.6) | copy-start | bytes 10616836
  6.5 83.5 %reduce-scatter.3.cloned.1.call-start = ((), (), s32[]{:S(2)}) async-start(), calls=%async_computation.3 | async-start | bytes 6291456 | tf_op jit(solution)/shard_map/reduce_scatter | solution.py:42
  39.9 1.0 copy-start.2
  41.7 13.7 %collective-permute-start = (bf16[1,64,16,128]{3,2,1,0:T(8,128)(2,1)}, bf16[1,64,16,128]{3,2,1,0:T(8,128)(2,1)}, u32[]{:S(2)}, u32[]{:S(2)}) collective-permute-start(bf16[1,64,16,128]{3,2,1,0:T(8,128)(2,1)} %bitcast.2), channel_id=1, source_target_pairs={{0,2},{2,4},{4,6},{6,8},{8,10},{10,12},{12,14},{1,3},{3,5},{5,7},{... | collective-permute-start | bytes 786440 | tf_op jit(solution)/shard_map/ppermute | solution.py:14
  45.7 9.6 %collective-permute-start.1 = (bf16[1,64,16,128]{3,2,1,0:T(8,128)(2,1)}, bf16[1,64,16,128]{3,2,1,0:T(8,128)(2,1)}, u32[]{:S(2)}, u32[]{:S(2)}) collective-permute-start(bf16[1,64,16,128]{3,2,1,0:T(8,128)(2,1)} %bitcast.5), channel_id=1, source_target_pairs={{2,0},{4,2},{6,4},{8,6},{10,8},{12,10},{14,12},{3,1},{5,3},{7,5},{... | collective-permute-start | bytes 786440 | tf_op jit(solution)/shard_map/ppermute | solution.py:15
  58.9 0.7 copy-start.6
  77.4 0.7 copy-start.4
  77.4 64.4 %reduce-scatter.5.cloned.1.call-start = ((), (), s32[]{:S(2)}) async-start(), calls=%async_computation.4 | async-start | bytes 6291456 | tf_op jit(solution)/shard_map/reduce_scatter | solution.py:42
  92.0 15.3 %collective-permute-start.2 = (bf16[1,64,16,128]{3,1,2,0:T(8,128)(2,1)S(1)}, bf16[1,64,16,128]{3,1,2,0:T(8,128)(2,1)S(1)}, u32[]{:S(2)}, u32[]{:S(2)}) collective-permute-start(bf16[1,64,16,128]{3,1,2,0:T(8,128)(2,1)S(1)} %get-tuple-element.5), channel_id=1, source_target_pairs={{0,2},{2,4},{4,6},{6,8},{8,10},{10,12},{12,14},{1,3},{3,5},{5,7},{... | collective-permute-start | bytes 786440 | tf_op jit(solution)/shard_map/ppermute | solution.py:14
  95.8 11.5 %collective-permute-start.3 = (bf16[1,64,16,128]{3,1,2,0:T(8,128)(2,1)S(1)}, bf16[1,64,16,128]{3,1,2,0:T(8,128)(2,1)S(1)}, u32[]{:S(2)}, u32[]{:S(2)}) collective-permute-start(bf16[1,64,16,128]{3,1,2,0:T(8,128)(2,1)S(1)} %get-tuple-element.6), channel_id=1, source_target_pairs={{2,0},{4,2},{6,4},{8,6},{10,8},{12,10},{14,12},{3,1},{5,3},{7,5},{... | collective-permute-start | bytes 786440 | tf_op jit(solution)/shard_map/ppermute | solution.py:15
  107.8 2.0 %copy-start.3 = (bf16[3,3,3,256,256]{4,3,2,1,0:T(8,128)(2,1)S(1)}, bf16[3,3,3,256,256]{4,3,2,1,0:T(8,128)(2,1)}, u32[]{:S(2)}) copy-start(bf16[3,3,3,256,256]{4,3,2,1,0:T(8,128)(2,1)} %param.8) | copy-start | bytes 10616836
  127.7 0.7 copy-start.5
  128.4 17.0 %copy-start.1 = (bf16[3,3,3,256,256]{4,3,2,1,0:T(8,128)(2,1)S(1)}, bf16[3,3,3,256,256]{4,3,2,1,0:T(8,128)(2,1)}, u32[]{:S(2)}) copy-start(bf16[3,3,3,256,256]{4,3,2,1,0:T(8,128)(2,1)} %param.6) | copy-start | bytes 10616836
Sparse Core Ops, SparseCore 0:
  77.6 12.4 reduce-scatter.2
  127.9 13.9 reduce-scatter.4
where the time goes:
time: 153 us; the launch traced here: 152 us
  waiting for transfers between devices  42.2 us (28%)
  blocking collectives  33.3 us (22%)
  matrix products  26.9 us (18%)
  local copies, waits for them, and re-layouts  20.4 us (13%)
  between operations  13.6 us (9%)
  starting transfers between devices  10.6 us (7%)
  other arithmetic  5.18 us (3%)
    all_to_all x1, blocking collectives, body(): lax.all_to_all(volume, 'space', split_axis=0, concat_axis=1, tiled=True)  33.3 us
    conv_general_dilated x2, matrix products, convolve(): lax.conv_general_dilated(field[None], kernel, (1, 1, 1), ((0, 0), (1, 1),...  26.9 us
    reduce_scatter x2, waiting for transfers between devices, layer(): lax.psum_scatter(convolve(field, part_kernel), 'chan', scatter_dimension=...  25.3 us
    ppermute x2, waiting for transfers between devices, padded(): before = lax.ppermute(last, axis, up)  17 us
    ppermute x2, starting transfers between devices, padded(): before = lax.ppermute(last, axis, up)  7.83 us
    conv_general_dilated x6, local copies, waits for them, and re-layouts, convolve(): lax.conv_general_dilated(field[None], kernel, (1, 1, 1), ((0, 0), (1, 1),...  7.73 us
    squeeze x2, local copies, waits for them, and re-layouts, convolve(): lax.conv_general_dilated(field[None], kernel, (1, 1, 1), ((0, 0), (1, 1),...  4.89 us
  transfers between devices with their start and end apart: 6, of which 4 were waited for; matrix products, arithmetic and copies ran while one was open for 1% of the time, Pallas kernels for 0%

commit v1 on v0

--- a/solution.py
+++ b/solution.py
@@ -2,6 +2,15 @@
 import jax.numpy as jnp
 from jax import lax
 from jax.sharding import PartitionSpec as P
+
+
+def use_ticks(raw, named_axis):
+    return jnp.concatenate(
+        lax.all_to_all(
+            jnp.stack(jnp.split(raw, lax.psum(1, named_axis), axis=0), axis=0), named_axis, 0, 0
+        ),
+        1,
+    )
 
 
 def padded(x, sides, width):
@@ -33,7 +42,7 @@
 
 
 def body(volume, weight_one, bias_one, weight_two, bias_two):
-    slab_data = lax.all_to_all(volume, "space", split_axis=0, concat_axis=1, tiled=True)
+    slab_data = use_ticks(volume, named_axis="space")
     share = slab_data.shape[3]
     offset = lax.axis_index("chan") * share
 

time: 153 us -> 160 us (1.046)
  local copies, waits for them, and re-layouts: 20.4 us -> 26.8 us
    unnamed x15 -> x22, local copies, waits for them, and re-layouts: 2.91 us -> 9.58 us
  transfers between devices with their start and end apart: 6 -> 6, of which waited for: 4 -> 4; matrix products, arithmetic and copies ran while one was open for 1% -> 0% of each run, Pallas kernels for 0% -> 0%
where the time goes in v1:
time: 160 us
  waiting for transfers between devices  43.6 us (27%)
  blocking collectives  32.8 us (20%)
  matrix products  26.9 us (17%)
  local copies, waits for them, and re-layouts  26.8 us (17%)
  between operations  13.6 us (8%)
  starting transfers between devices  10.6 us (7%)
  other arithmetic  5.49 us (3%)
    all_to_all x1, blocking collectives, use_ticks(): lax.all_to_all(jnp.stack(jnp.split(raw, lax.psum(1, named_axis), axis=0),...  32.8 us
    conv_general_dilated x2, matrix products, convolve(): lax.conv_general_dilated(field[None], kernel, (1, 1, 1), ((0, 0), (1, 1),...  26.9 us
    reduce_scatter x2, waiting for transfers between devices, layer(): lax.psum_scatter(convolve(field, part_kernel), 'chan', scatter_dimension=...  25.2 us
    ppermute x2, waiting for transfers between devices, padded(): before = lax.ppermute(last, axis, up)  18.4 us
    unnamed x22, local copies, waits for them, and re-layouts  9.58 us
    ppermute x2, starting transfers between devices, padded(): before = lax.ppermute(last, axis, up)  7.83 us
    conv_general_dilated x6, local copies, waits for them, and re-layouts, convolve(): lax.conv_general_dilated(field[None], kernel, (1, 1, 1), ((0, 0), (1, 1),...  7.73 us
    squeeze x2, local copies, waits for them, and re-layouts, convolve(): lax.conv_general_dilated(field[None], kernel, (1, 1, 1), ((0, 0), (1, 1),...  4.89 us
  transfers between devices with their start and end apart: 6, of which 4 were waited for; matrix products, arithmetic and copies ran while one was open for 0% of the time, Pallas kernels for 0%

profile of v1, /device:TPU:0, one launch (start us, length us, event | category | flops | bytes accessed | tf_op | source)
XLA Modules:
  0.0 160.0 jit_solution(14186295855541255679)
XLA Ops:
  6.5 1.1 bitcast_dynamic-update-slice_fusion.7
  7.6 1.0 bitcast_dynamic-update-slice_fusion.6
  14.2 32.8 %all_to_all.5 = bf16[8,4,8,16,128]{4,3,2,1,0:T(8,128)(2,1)S(1)} all-to-all(bf16[8,4,8,16,128]{4,3,2,1,0:T(8,128)(2,1)S(1)} %bitcast_dynamic-update-slice_fusion), channel_id=1, replica_groups=mesh['tiles'=2,'space'=8,'chan'=2] {'space'}, dimensions={0} | all-to-all | bytes 2097152 | tf_op jit(solution)/shard_map/all_to_all | solution.py:9
  47.3 1.0 copy-done.2
  49.1 4.1 %collective-permute-start = (bf16[1,64,16,128]{3,2,1,0:T(8,128)(2,1)}, bf16[1,64,16,128]{3,2,1,0:T(8,128)(2,1)}, u32[]{:S(2)}, u32[]{:S(2)}) collective-permute-start(bf16[1,64,16,128]{3,2,1,0:T(8,128)(2,1)} %bitcast.9), channel_id=1, source_target_pairs={{0,2},{2,4},{4,6},{6,8},{8,10},{10,12},{12,14},{1,3},{3,5},{5,7},{... | collective-permute-start | bytes 786440 | tf_op jit(solution)/shard_map/ppermute | solution.py:23
  53.2 1.3 collective-permute-start.1
  54.5 8.3 %collective-permute-done = bf16[1,64,16,128]{3,2,1,0:T(8,128)(2,1)} collective-permute-done((bf16[1,64,16,128]{3,2,1,0:T(8,128)(2,1)}, bf16[1,64,16,128]{3,2,1,0:T(8,128)(2,1)}, u32[]{:S(2)}, u32[]{:S(2)}) %collective-permute-start) | collective-permute-done | bytes 262176 | tf_op jit(solution)/shard_map/ppermute | solution.py:23
  62.8 1.5 maximum_bitcast_fusion
  65.2 1.5 copy.17
  67.4 13.5 %broadcast_select_fusion.1 = f32[4,64,8,3,256]{4,2,3,1,0:T(8,128)S(1)} fusion(pred[8,3]{0,1:T(4,128)(4,1)S(1)} %copy-done.6, bf16[6,64,1,7,2,128]{5,3,4,1,0,2:T(8,128)(2,1)S(1)} %slice.30, bf16[6,64,1,8,3,128]{5,3,4,1,0,2:T(8,128)(2,1)S(1)} %copy.17, bf16[3,3,3,256,256]{4,3,2,1,0:T(8,128)(2,1)S(1)} %copy-done, s32[]{:T(128)S(6)} %select_n.2), kind=kOutput, calls=%fused_computation.18 | convolution fusion | flops 10771759104 | bytes 11993604 | tf_op jit(solution)/shard_map/conv_general_dilated | solution.py:30
  80.8 1.9 %copy.18 = f32[4,64,8,3,256]{4,1,3,2,0:T(8,128)S(1)} copy(f32[4,64,8,3,256]{4,2,3,1,0:T(8,128)S(1)} %broadcast_select_fusion.1) | data formatting | bytes 12582912 | tf_op jit(solution)/shard_map/conv_general_dilated | solution.py:30
  82.7 2.4 %slice_bitcast_fusion.1 = f32[4,64,16,256]{3,1,2,0:T(8,128)} fusion(f32[4,64,1,24,256]{4,1,3,0,2:T(8,128)S(1)} %bitcast.44), kind=kLoop, calls=%fused_computation.4 | loop fusion | bytes 8388608 | tf_op jit(solution)/shard_map/squeeze | solution.py:30
  85.9 11.9 %reduce-scatter.3.cloned.1.call-done = f32[4,64,16,128]{3,1,2,0:T(8,128)} async-done(((f32[4,64,16,256]{3,1,2,0:T(8,128)}), f32[4,64,16,128]{3,1,2,0:T(8,128)}) %reduce-scatter.3.cloned.1.call-update) | async-done | bytes 2097168 | tf_op jit(solution)/shard_map/reduce_scatter | solution.py:51
  97.8 1.9 %maximum_convert_fusion.1 = bf16[4,64,16,128]{3,1,2,0:T(8,128)(2,1)S(1)} fusion(f32[4,64,16,128]{3,1,2,0:T(8,128)} %reduce-scatter.3.cloned.1.call-done, f32[128]{0:T(128)S(1)} %dynamic_slice.13), kind=kLoop, calls=%fused_computation.20 | loop fusion | flops 1572864 | bytes 3146240 | tf_op jit(solution)/shard_map/convert_element_type | solution.py:56
  99.8 3.8 %collective-permute-start.2 = (bf16[1,64,16,128]{3,1,2,0:T(8,128)(2,1)S(1)}, bf16[1,64,16,128]{3,1,2,0:T(8,128)(2,1)S(1)}, u32[]{:S(2)}, u32[]{:S(2)}) collective-permute-start(bf16[1,64,16,128]{3,1,2,0:T(8,128)(2,1)S(1)} %get-tuple-element.5), channel_id=1, source_target_pairs={{0,2},{2,4},{4,6},{6,8},{8,10},{10,12},{12,14},{1,3},{3,5},{5,7},{... | collective-permute-start | bytes 786440 | tf_op jit(solution)/shard_map/ppermute | solution.py:23
  103.5 1.5 collective-permute-start.3
  105.0 10.0 %collective-permute-done.2 = bf16[1,64,16,128]{3,1,2,0:T(8,128)(2,1)S(1)} collective-permute-done((bf16[1,64,16,128]{3,1,2,0:T(8,128)(2,1)S(1)}, bf16[1,64,16,128]{3,1,2,0:T(8,128)(2,1)S(1)}, u32[]{:S(2)}, u32[]{:S(2)}) %collective-permute-start.2) | collective-permute-done | bytes 262176 | tf_op jit(solution)/shard_map/ppermute | solution.py:23
  115.6 1.5 copy.20
  117.6 13.5 %broadcast_select_fusion = f32[4,64,8,3,256]{4,2,3,1,0:T(8,128)S(1)} fusion(pred[8,3]{0,1:T(4,128)(4,1)S(1)} %copy-done.6, bf16[6,64,1,7,2,128]{5,3,4,1,0,2:T(8,128)(2,1)S(1)} %slice.34, bf16[6,64,1,8,3,128]{5,3,4,1,0,2:T(8,128)(2,1)S(1)} %copy.20, bf16[3,3,3,256,256]{4,3,2,1,0:T(8,128)(2,1)S(1)} %copy-done.3, s32[]{:T(128)S(6)} %select_n.2), kind=kOutput, calls=%fused_computation.17 | convolution fusion | flops 10771759104 | bytes 11993604 | tf_op jit(solution)/shard_map/conv_general_dilated | solution.py:30
  131.1 1.9 %copy.21 = f32[4,64,8,3,256]{4,1,3,2,0:T(8,128)S(1)} copy(f32[4,64,8,3,256]{4,2,3,1,0:T(8,128)S(1)} %broadcast_select_fusion) | data formatting | bytes 12582912 | tf_op jit(solution)/shard_map/conv_general_dilated | solution.py:30
  133.1 2.4 %slice_bitcast_fusion = f32[4,64,16,256]{3,1,2,0:T(8,128)} fusion(f32[4,64,1,24,256]{4,1,3,0,2:T(8,128)S(1)} %bitcast.45), kind=kLoop, calls=%fused_computation.3 | loop fusion | bytes 8388608 | tf_op jit(solution)/shard_map/squeeze | solution.py:30
  136.3 13.3 %reduce-scatter.5.cloned.1.call-done = f32[4,64,16,128]{3,1,2,0:T(8,128)} async-done(((f32[4,64,16,256]{3,1,2,0:T(8,128)}), f32[4,64,16,128]{3,1,2,0:T(8,128)}) %reduce-scatter.5.cloned.1.call-update) | async-done | bytes 2097168 | tf_op jit(solution)/shard_map/reduce_scatter | solution.py:51
  149.6 1.9 %maximum_convert_fusion = bf16[4,64,16,128]{3,1,2,0:T(8,128)(2,1)S(1)} fusion(f32[4,64,16,128]{3,1,2,0:T(8,128)} %reduce-scatter.5.cloned.1.call-done, f32[128]{0:T(128)S(1)} %dynamic_slice.15), kind=kLoop, calls=%fused_computation.19 | loop fusion | flops 1572864 | bytes 3146240 | tf_op jit(solution)/shard_map/convert_element_type | solution.py:60
  151.5 1.7 %copy.22 = bf16[4,64,16,128]{3,2,1,0:T(8,128)(2,1)} copy(bf16[4,64,16,128]{3,1,2,0:T(8,128)(2,1)S(1)} %maximum_convert_fusion) | data formatting | bytes 2097152 | tf_op jit(solution)/shard_map/convert_element_type | solution.py:60
  (36 shorter events, 10.6 us)
Async XLA Ops:
  6.5 60.6 %copy-start = (bf16[3,3,3,256,256]{4,3,2,1,0:T(8,128)(2,1)S(1)}, bf16[3,3,3,256,256]{4,3,2,1,0:T(8,128)(2,1)}, u32[]{:S(2)}) copy-start(bf16[3,3,3,256,256]{4,3,2,1,0:T(8,128)(2,1)} %param.6) | copy-start | bytes 10616836
  6.5 91.3 %reduce-scatter.3.cloned.1.call-start = ((), (), s32[]{:S(2)}) async-start(), calls=%async_computation.3 | async-start | bytes 6291456 | tf_op jit(solution)/shard_map/reduce_scatter | solution.py:51
  47.3 1.0 copy-start.2
  49.1 13.7 %collective-permute-start = (bf16[1,64,16,128]{3,2,1,0:T(8,128)(2,1)}, bf16[1,64,16,128]{3,2,1,0:T(8,128)(2,1)}, u32[]{:S(2)}, u32[]{:S(2)}) collective-permute-start(bf16[1,64,16,128]{3,2,1,0:T(8,128)(2,1)} %bitcast.9), channel_id=1, source_target_pairs={{0,2},{2,4},{4,6},{6,8},{8,10},{10,12},{12,14},{1,3},{3,5},{5,7},{... | collective-permute-start | bytes 786440 | tf_op jit(solution)/shard_map/ppermute | solution.py:23
  53.2 9.6 %collective-permute-start.1 = (bf16[1,64,16,128]{3,2,1,0:T(8,128)(2,1)}, bf16[1,64,16,128]{3,2,1,0:T(8,128)(2,1)}, u32[]{:S(2)}, u32[]{:S(2)}) collective-permute-start(bf16[1,64,16,128]{3,2,1,0:T(8,128)(2,1)} %bitcast.11), channel_id=1, source_target_pairs={{2,0},{4,2},{6,4},{8,6},{10,8},{12,10},{14,12},{3,1},{5,3},{7,5},{... | collective-permute-start | bytes 786440 | tf_op jit(solution)/shard_map/ppermute | solution.py:24
  66.7 0.7 copy-start.6
  85.2 0.7 copy-start.4
  85.2 64.4 %reduce-scatter.5.cloned.1.call-start = ((), (), s32[]{:S(2)}) async-start(), calls=%async_computation.4 | async-start | bytes 6291456 | tf_op jit(solution)/shard_map/reduce_scatter | solution.py:51
  99.8 15.3 %collective-permute-start.2 = (bf16[1,64,16,128]{3,1,2,0:T(8,128)(2,1)S(1)}, bf16[1,64,16,128]{3,1,2,0:T(8,128)(2,1)S(1)}, u32[]{:S(2)}, u32[]{:S(2)}) collective-permute-start(bf16[1,64,16,128]{3,1,2,0:T(8,128)(2,1)S(1)} %get-tuple-element.5), channel_id=1, source_target_pairs={{0,2},{2,4},{4,6},{6,8},{8,10},{10,12},{12,14},{1,3},{3,5},{5,7},{... | collective-permute-start | bytes 786440 | tf_op jit(solution)/shard_map/ppermute | solution.py:23
  103.5 11.5 %collective-permute-start.3 = (bf16[1,64,16,128]{3,1,2,0:T(8,128)(2,1)S(1)}, bf16[1,64,16,128]{3,1,2,0:T(8,128)(2,1)S(1)}, u32[]{:S(2)}, u32[]{:S(2)}) collective-permute-start(bf16[1,64,16,128]{3,1,2,0:T(8,128)(2,1)S(1)} %get-tuple-element.6), channel_id=1, source_target_pairs={{2,0},{4,2},{6,4},{8,6},{10,8},{12,10},{14,12},{3,1},{5,3},{7,5},{... | collective-permute-start | bytes 786440 | tf_op jit(solution)/shard_map/ppermute | solution.py:24
  115.6 2.0 %copy-start.3 = (bf16[3,3,3,256,256]{4,3,2,1,0:T(8,128)(2,1)S(1)}, bf16[3,3,3,256,256]{4,3,2,1,0:T(8,128)(2,1)}, u32[]{:S(2)}) copy-start(bf16[3,3,3,256,256]{4,3,2,1,0:T(8,128)(2,1)} %param.8) | copy-start | bytes 10616836
  135.5 0.7 copy-start.5
  136.2 17.0 %copy-start.1 = (bf16[3,3,3,256,256]{4,3,2,1,0:T(8,128)(2,1)S(1)}, bf16[3,3,3,256,256]{4,3,2,1,0:T(8,128)(2,1)}, u32[]{:S(2)}) copy-start(bf16[3,3,3,256,256]{4,3,2,1,0:T(8,128)(2,1)} %param.6) | copy-start | bytes 10616836
Sparse Core Ops, SparseCore 0:
  85.3 12.4 reduce-scatter.2
  135.6 13.8 reduce-scatter.4
